TPU v7x, 256 devices: a whole 4x4x8 slice. The times are simulated.
256 devices in a mesh: seq: 64 (over z, x, core), tp: 4 (over y).
Axes of the slice: x: 4, y: 4, z: 8, core: 2. Of those that a mesh axis runs over, the one named last changes fastest.
Arguments:
- tokens: bfloat16 [32768, 2048], P('seq', 'tp'), may hold values from -6 to 6
- norm_gain: float32 [2048], replicated, may hold values from 0.1 to 1.9
- w_query: bfloat16 [2048, 2048], P(None, 'tp'), may hold values from -0.125 to 0.125
- w_keyval: bfloat16 [2048, 256], replicated, may hold values from -0.125 to 0.125
- w_out: bfloat16 [2048, 2048], P('tp'), may hold values from -0.5 to 0.5
- span_lens: int32 [64], P('seq'), may hold values from 1 to 512, 24576 in all
- cached_lens: int32 [64], P('seq'), may hold values from 1 to 1536, 49152 in all
- old_table: int32 [64, 64], P('seq'), may hold values from 0 to 63, each once within a row
- new_table: int32 [64, 64], P('seq'), may hold values from 0 to 63, each once within a row
- old_cache: bfloat16 [4096, 32, 256], P('seq', 'tp'), may hold values from -720 to 720
Outputs:
- mixed: bfloat16 [32768, 2048], P('seq', 'tp')
- new_cache: bfloat16 [4096, 32, 256], P('seq', 'tp')
Inputs may be any that keep to these rules, and one draw needn't show every extreme that they name: Request r's new tokens are the first span_lens[r] of its 512 rows. `old_table`: each row names every device once: each device holds exactly one block of every request. `new_table`: each row names every device once: each device receives exactly one block of every request.
All inputs are finite; a program needn't handle non-finite values. No bound on the sum of `span_lens` or of `cached_lens` on one device may be relied on, other than what follows from the above.
Results may differ from a plain program's by a relative error of at most 0.012.
The roundings to bfloat16 on the way count: a program that leaves them out, or rounds other values in their place, can miss the bound.
Values may be sent and summed in bfloat16 or wider, within the bound.
A program may use at most 128 MiB of HBM per device.

v0:
```python
import jax
import jax.numpy as jnp
from jax import lax
from jax.sharding import PartitionSpec as P

EPSILON = 1e-05
MASKED = -1e30


def normalize(rows, norm_gain):
    values = rows.astype(jnp.float32)
    average = jnp.mean(values, axis=1, keepdims=True)
    centred = values - average
    spread = jnp.mean(centred * centred, axis=1, keepdims=True)
    return (centred * lax.rsqrt(spread + EPSILON) * norm_gain).astype(jnp.bfloat16)


def body(
    tokens,
    norm_gain,
    w_query,
    w_keyval,
    w_out,
    span_lens,
    cached_lens,
    old_table,
    new_table,
    old_cache,
):
    groups = lax.axis_size("seq")
    tp_count = lax.axis_size("tp")
    tp_index = lax.axis_index("tp")
    holders = old_table[0]
    held_len = cached_lens[0]
    span_len = span_lens[0]
    tok_rows = tokens.shape[0]
    share = old_cache.shape[1]
    width = old_cache.shape[2]
    block_rows = share * tp_count
    capacity = groups * block_rows
    arrived = lax.all_to_all(old_cache, "seq", split_axis=0, concat_axis=0, tiled=True)
    cache_share = jnp.take(arrived, holders, axis=0)
    full_rows = lax.all_gather(tokens, "tp", axis=1, tiled=True)
    normed = normalize(full_rows, norm_gain)
    query = jnp.dot(normed, w_query, preferred_element_type=jnp.float32).astype(jnp.bfloat16)
    keyval = jnp.dot(normed, w_keyval, preferred_element_type=jnp.float32).astype(jnp.bfloat16)
    shifted = lax.dynamic_update_slice(
        jnp.zeros((capacity, width), jnp.bfloat16), keyval, (held_len, jnp.int32(0))
    )
    shifted_share = lax.dynamic_slice_in_dim(
        shifted.reshape(groups, block_rows, width), tp_index * share, share, 1
    )
    share_pos = (
        lax.broadcasted_iota(jnp.int32, (groups, share, 1), 0) * block_rows
        + tp_index * share
        + lax.broadcasted_iota(jnp.int32, (groups, share, 1), 1)
    )
    fresh_share = jnp.where(
        share_pos < held_len,
        cache_share,
        jnp.where(share_pos < held_len + span_len, shifted_share, jnp.zeros_like(shifted_share)),
    )
    targets = new_table[0]
    device_ids = lax.broadcasted_iota(jnp.int32, (groups, groups), 0)
    block_ids = lax.broadcasted_iota(jnp.int32, (groups, groups), 1)
    matches = targets[None, :] == device_ids
    sources = jnp.sum(jnp.where(matches, block_ids, 0), axis=1)
    new_cache = lax.all_to_all(
        jnp.take(fresh_share, sources, axis=0), "seq", split_axis=0, concat_axis=0, tiled=True
    )
    cached = lax.all_gather(cache_share, "tp", axis=1, tiled=True).reshape(capacity, width)
    positions = lax.broadcasted_iota(jnp.int32, (capacity, 1), 0)
    fresh = jnp.where(
        positions < held_len,
        cached,
        jnp.where(positions < held_len + span_len, shifted, jnp.zeros_like(shifted)),
    )
    head_size = width // 2
    keys = fresh[:, :head_size]
    values = fresh[:, head_size:]
    local_heads = query.shape[1] // head_size
    query3 = query.reshape(tok_rows, local_heads, head_size)
    scores = jnp.einsum(
        "thd,kd->htk", query3, keys, preferred_element_type=jnp.float32
    ) * head_size ** (-0.5)
    row_pos = lax.broadcasted_iota(jnp.int32, (tok_rows, 1), 0)
    key_pos = lax.broadcasted_iota(jnp.int32, (1, capacity), 1)
    allowed = key_pos <= held_len + row_pos
    scores = jnp.where(allowed[None], scores, MASKED)
    top = jnp.max(scores, axis=2, keepdims=True)
    weights = jnp.exp(scores - top)
    probs = (weights / jnp.sum(weights, axis=2, keepdims=True)).astype(jnp.bfloat16)
    context = jnp.einsum("htk,kd->thd", probs, values, preferred_element_type=jnp.float32).astype(
        jnp.bfloat16
    )
    context = context.reshape(tok_rows, local_heads * head_size)
    partial_out = jnp.dot(context, w_out, preferred_element_type=jnp.float32)
    summed = lax.psum_scatter(
        partial_out.astype(jnp.bfloat16), "tp", scatter_dimension=1, tiled=True
    ).astype(jnp.float32)
    total = tokens.astype(jnp.float32) + summed
    mixed = jnp.where(row_pos < span_len, total, jnp.zeros_like(total)).astype(jnp.bfloat16)
    return (mixed, new_cache)


def solution(mesh):
    in_specs = (
        P("seq", "tp"),
        P(),
        P(None, "tp"),
        P(),
        P("tp", None),
        P("seq"),
        P("seq"),
        P("seq", None),
        P("seq", None),
        P("seq", "tp", None),
    )
    out_specs = (P("seq", "tp"), P("seq", "tp", None))
    return jax.shard_map(body, mesh=mesh, in_specs=in_specs, out_specs=out_specs, check_vma=False)
```

profile of v0, /device:TPU:1, one launch (start us, length us, event | category | flops | bytes accessed | tf_op | source)
XLA Modules:
  0.0 153.1 jit_solution(9230389170875504754)
XLA Ops:
  7.2 0.7 all-gather.5.cloned.1.call-update
  7.9 13.0 %all-to-all-start = ((bf16[64,8,256]{2,1,0:T(8,128)(2,1)}), bf16[64,8,256]{2,1,0:T(8,128)(2,1)S(1)}, u32[]{:S(2)}, u32[]{:S(2)}) async-start(bf16[64,8,256]{2,1,0:T(8,128)(2,1)} %param.21), calls=%async_computation | async-start | bytes 524288 | tf_op jit(solution)/shard_map/all_to_all | solution.py:41
  22.3 0.7 compare_select_fusion.1
  23.0 0.7 compare_and_fusion.1
  23.6 0.1 fusion.16
  23.7 10.4 %all-to-all-done = bf16[64,8,256]{2,1,0:T(8,128)(2,1)S(1)} async-done(((bf16[64,8,256]{2,1,0:T(8,128)(2,1)}), bf16[64,8,256]{2,1,0:T(8,128)(2,1)S(1)}, u32[]{:S(2)}, u32[]{:S(2)}) %all-to-all-start) | async-done | bytes 262176 | tf_op jit(solution)/shard_map/all_to_all | solution.py:41
  34.1 1.3 gather_fusion
  35.4 11.7 %all-gather.5.cloned.1.call-done = bf16[512,2048]{1,0:T(8,128)(2,1)} async-done(((bf16[512,512]{1,0:T(8,128)(2,1)}), bf16[512,2048]{1,0:T(8,128)(2,1)}) %all-gather.5.cloned.1.call-update) | async-done | bytes 2097168 | tf_op jit(solution)/shard_map/all_gather | solution.py:43
  47.1 2.1 %convert_reduce_fusion = f32[512]{0:T(512)S(1)} fusion(bf16[512,2048]{1,0:T(8,128)(2,1)} %all-gather.5.cloned.1.call-done), kind=kLoop, calls=%fused_computation.12 | loop fusion | flops 2096640 | bytes 2099200 | tf_op jit(solution)/shard_map/reduce_sum | solution.py:12
  49.2 2.3 %fusion.8 = f32[512]{0:T(512)S(1)} fusion(bf16[512,2048]{1,0:T(8,128)(2,1)} %all-gather.5.cloned.1.call-done, f32[512]{0:T(512)S(1)} %broadcast_multiply_fusion), kind=kLoop, calls=%fused_computation.15 | loop fusion | flops 4193792 | bytes 2101248 | tf_op jit(solution)/shard_map/reduce_sum | solution.py:14
  51.5 0.7 fusion.10
  52.3 0.7 convolution_convert_fusion.2
  53.0 0.6 copy-done.2
  53.6 0.1 broadcast.104
  53.7 1.9 %dynamic_update_slice.3 = bf16[2048,256]{1,0:T(8,128)(2,1)S(1)} dynamic-update-slice(bf16[2048,256]{1,0:T(8,128)(2,1)S(1)} %broadcast.104, bf16[512,256]{1,0:T(8,128)(2,1)S(1)} %convolution_convert_fusion.2, s32[]{:T(128)S(6)} %select_n.39, s32[]{:T(128)} %constant.9.clone.1) | dynamic-update-slice | bytes 524292 | tf_op jit(solution)/shard_map/dynamic_update_slice | solution.py:47
  55.6 1.9 %select_select_fusion = (bf16[64,8,256]{2,1,0:T(8,128)(2,1)S(1)}, bf16[64,8,256]{2,1,0:T(8,128)(2,1)}) fusion(bf16[64,32,256]{2,1,0:T(8,128)(2,1)S(1)} %bitcast.57, s32[]{:T(128)S(6)} %select_n.44, pred[64,8]{1,0:T(8,128)(4,1)S(1)} %get-tuple-element.6, pred[64,8]{1,0:T(8,128)(4,1)S(1)} %get-tuple-element.5, bf16[64,8,256]{2,1,0:T(8,128)(2,1)} %gather_fusion, ...), kind=kLoop, calls=%fused_computation.29 | loop fusion | flops 393216 | bytes 1049668 | tf_op jit(solution)/shard_map/jit(_where)/select_n | solution.py:58
  57.5 0.2 reduce-scatter.2.cloned.1.call-start
  57.8 1.8 %iota_compare_fusion = pred[512,2048]{0,1:T(8,128)(4,1)} fusion(s32[512]{0:T(512)S(1)} %iota_add_fusion.1), kind=kLoop, calls=%fused_computation.18 | loop fusion | flops 1048576 | bytes 1050624 | tf_op jit(solution)/shard_map/le | solution.py:88
  59.6 4.3 %convolution_convert_fusion.1 = bf16[512,512]{0,1:T(8,128)(2,1)} fusion(bf16[512,2048]{1,0:T(8,128)(2,1)} %copy-done.2, bf16[2048,512]{1,0:T(8,128)(2,1)} %param.14), kind=kOutput, calls=%fused_computation.21 | convolution fusion | flops 1074003968 | bytes 4718592 | tf_op jit(solution)/shard_map/dot_general | solution.py:45
  63.9 21.4 %all-gather.3.cloned.1.call-done = bf16[64,32,256]{2,1,0:T(8,128)(2,1)} async-done(((bf16[64,8,256]{2,1,0:T(8,128)(2,1)}), bf16[64,32,256]{2,1,0:T(8,128)(2,1)}) %all-gather.3.cloned.1.call-update) | async-done | bytes 1048592 | tf_op jit(solution)/shard_map/all_gather | solution.py:71
  85.3 3.8 %bitcast_select_fusion.4 = bf16[2048,256]{1,0:T(8,128)(2,1)} fusion(bf16[64,32,256]{2,1,0:T(8,128)(2,1)} %all-gather.3.cloned.1.call-done, bf16[2048,256]{1,0:T(8,128)(2,1)S(1)} %dynamic_update_slice.3, pred[2048]{0:T(1024)(128)(4,1)S(1)} %get-tuple-element.9, pred[2048]{0:T(1024)(128)(4,1)S(1)} %get-tuple-element.10), kind=kLoop, calls=%fused_computation.24 | loop fusion | flops 1048576 | bytes 3149824 | tf_op jit(solution)/shard_map/jit(_where)/select_n | solution.py:73
  89.1 10.7 %fusion.19 = (f32[4,512]{1,0:T(4,128)S(1)}, f32[4,512,2048]{1,2,0:T(8,128)}) fusion(pred[512,2048]{0,1:T(8,128)(4,1)} %iota_compare_fusion, bf16[512,4,128]{0,2,1:T(8,128)(2,1)} %bitcast.59, bf16[2048,256]{1,0:T(8,128)(2,1)} %bitcast_select_fusion.4), kind=kOutput, calls=%fused_computation.52 | convolution fusion | flops 1090521088 | bytes 18882560 | tf_op jit(solution)/shard_map/sub | solution.py:91
  99.8 7.0 %fusion.13 = bf16[128,4,512]{2,0,1:T(8,128)(2,1)S(1)} fusion(f32[4,512,2048]{1,2,0:T(8,128)} %get-tuple-element.8, f32[4,512]{1,0:T(4,128)S(1)} %get-tuple-element.7, bf16[2048,256]{1,0:T(8,128)(2,1)S(1)} %copy-done.4), kind=kOutput, calls=%fused_computation.22 | convolution fusion | flops 1082392576 | bytes 17833984 | tf_op jit(solution)/shard_map/htk,kd->thd/dot_general | solution.py:93
  106.9 2.6 %convolution_convert_fusion = bf16[512,2048]{1,0:T(8,128)(2,1)} fusion(bf16[512,512]{0,1:T(8,128)(2,1)S(1)} %bitcast.60, bf16[512,2048]{1,0:T(8,128)(2,1)S(1)} %copy-done), kind=kOutput, calls=%fused_computation.19 | convolution fusion | flops 1074790400 | bytes 4718592 | tf_op jit(solution)/shard_map/dot_general | solution.py:97
  109.5 0.1 select_reduce_fusion
  109.7 0.6 gather_fusion.1
  110.3 0.8 broadcast_select_fusion
  111.1 11.5 %all-to-all-start.1 = ((bf16[64,8,256]{2,1,0:T(8,128)(2,1)}), bf16[64,8,256]{2,1,0:T(8,128)(2,1)S(1)}, u32[]{:S(2)}, u32[]{:S(2)}) async-start(bf16[64,8,256]{2,1,0:T(8,128)(2,1)} %broadcast_select_fusion), calls=%async_computation.2 | async-start | bytes 524288 | tf_op jit(solution)/shard_map/all_to_all | solution.py:68
  122.7 13.1 %all-to-all-done.1 = bf16[64,8,256]{2,1,0:T(8,128)(2,1)S(1)} async-done(((bf16[64,8,256]{2,1,0:T(8,128)(2,1)}), bf16[64,8,256]{2,1,0:T(8,128)(2,1)S(1)}, u32[]{:S(2)}, u32[]{:S(2)}) %all-to-all-start.1) | async-done | bytes 262176 | tf_op jit(solution)/shard_map/all_to_all | solution.py:68
  135.8 8.0 %reduce-scatter.2.cloned.1.call-done = bf16[512,512]{1,0:T(8,128)(2,1)} async-done(((bf16[512,2048]{1,0:T(8,128)(2,1)}), bf16[512,512]{1,0:T(8,128)(2,1)}) %reduce-scatter.2.cloned.1.call-update) | async-done | bytes 524304 | tf_op jit(solution)/shard_map/reduce_scatter | solution.py:98
  143.8 2.0 %select_convert_fusion = bf16[512,512]{1,0:T(8,128)(2,1)} fusion(bf16[512,512]{1,0:T(8,128)(2,1)} %reduce-scatter.2.cloned.1.call-done, bf16[512,512]{1,0:T(8,128)(2,1)S(1)} %copy-done.3, pred[512]{0:T(512)(128)(4,1)S(1)} %iota_compare_fusion.4), kind=kLoop, calls=%fused_computation.25 | loop fusion | flops 1310720 | bytes 1573376 | tf_op jit(solution)/shard_map/convert_element_type | solution.py:102
  145.9 0.7 copy.29
  (29 shorter events, 0.2 us)
Async XLA Ops:
  7.2 99.7 %copy-start = (bf16[512,2048]{1,0:T(8,128)(2,1)S(1)}, bf16[512,2048]{1,0:T(8,128)(2,1)}, u32[]{:S(2)}) copy-start(bf16[512,2048]{1,0:T(8,128)(2,1)} %param.16) | copy-start | bytes 6291460
  7.2 44.3 %copy-start.5 = (f32[2048]{0:T(1024)S(1)}, f32[2048]{0:T(1024)}, u32[]{:S(2)}) copy-start(f32[2048]{0:T(1024)} %param.13) | copy-start | bytes 24580
  7.2 39.9 %all-gather.5.cloned.1.call-start = ((), (), s32[]{:S(2)}) async-start(), calls=%async_computation.4 | async-start | bytes 2621440 | tf_op jit(solution)/shard_map/all_gather | solution.py:43
  7.9 26.2 %all-to-all-start = ((bf16[64,8,256]{2,1,0:T(8,128)(2,1)}), bf16[64,8,256]{2,1,0:T(8,128)(2,1)S(1)}, u32[]{:S(2)}, u32[]{:S(2)}) async-start(bf16[64,8,256]{2,1,0:T(8,128)(2,1)} %param.21), calls=%async_computation | async-start | bytes 524288 | tf_op jit(solution)/shard_map/all_to_all | solution.py:41
  20.9 64.3 %all-gather.3.cloned.1.call-start = ((), (), s32[]{:S(2)}) async-start(), calls=%async_computation.3 | async-start | bytes 1310720 | tf_op jit(solution)/shard_map/all_gather | solution.py:71
  47.1 4.4 %copy-start.1 = (bf16[512,2048]{1,0:T(8,128)(2,1)S(1)}, bf16[512,2048]{1,0:T(8,128)(2,1)}, u32[]{:S(2)}) copy-start(bf16[512,2048]{1,0:T(8,128)(2,1)} %all-gather.5.cloned.1.call-done) | copy-start | bytes 6291460
  47.1 5.1 %copy-start.6 = (bf16[2048,256]{1,0:T(8,128)(2,1)S(1)}, bf16[2048,256]{1,0:T(8,128)(2,1)}, u32[]{:S(2)}) copy-start(bf16[2048,256]{1,0:T(8,128)(2,1)} %param.15) | copy-start | bytes 3145732
  52.3 1.3 copy-start.2
  57.5 86.3 %reduce-scatter.2.cloned.1.call-start = ((), (), s32[]{:S(2)}) async-start(), calls=%async_computation.5 | async-start | bytes 2621440 | tf_op jit(solution)/shard_map/reduce_scatter | solution.py:98
  89.1 10.7 %copy-start.4 = (bf16[2048,256]{1,0:T(8,128)(2,1)S(1)}, bf16[2048,256]{1,0:T(8,128)(2,1)}, u32[]{:S(2)}) copy-start(bf16[2048,256]{1,0:T(8,128)(2,1)} %bitcast_select_fusion.4) | copy-start | bytes 3145732
  106.8 2.7 %copy-start.7 = (s32[1,64]{1,0:T(1,128)S(1)}, s32[1,64]{1,0:T(1,128)}, u32[]{:S(2)}) copy-start(s32[1,64]{1,0:T(1,128)} %param.20) | copy-start | bytes 772
  106.9 37.0 %copy-start.3 = (bf16[512,512]{1,0:T(8,128)(2,1)S(1)}, bf16[512,512]{1,0:T(8,128)(2,1)}, u32[]{:S(2)}) copy-start(bf16[512,512]{1,0:T(8,128)(2,1)} %param.12) | copy-start | bytes 1572868
  111.1 24.7 %all-to-all-start.1 = ((bf16[64,8,256]{2,1,0:T(8,128)(2,1)}), bf16[64,8,256]{2,1,0:T(8,128)(2,1)S(1)}, u32[]{:S(2)}, u32[]{:S(2)}) async-start(bf16[64,8,256]{2,1,0:T(8,128)(2,1)} %broadcast_select_fusion), calls=%async_computation.2 | async-start | bytes 524288 | tf_op jit(solution)/shard_map/all_to_all | solution.py:68
Sparse Core Ops, SparseCore 0:
  9.8 37.2 all-gather.4
  57.6 27.5 all-gather.2
  109.6 34.1 reduce-scatter.1
where the time goes:
time: 154 us; the launch traced here: 153 us
  waiting for transfers between devices  65.4 us (42%)
  matrix products  25.4 us (16%)
  starting transfers between devices  24.8 us (16%)
  other arithmetic  17 us (11%)
  between operations  15.3 us (10%)
  local copies, waits for them, and re-layouts  5.21 us (3%)
    all_gather x1, waiting for transfers between devices, body(): lax.all_gather(cache_share, 'tp', axis=1, tiled=True)  21.4 us
    all_to_all x1, waiting for transfers between devices, body(): lax.all_to_all(jnp.take(fresh_share, sources, axis=0), 'seq', split_axis=...  13.1 us
    all_to_all x1, starting transfers between devices, body(): lax.all_to_all(old_cache, 'seq', split_axis=0, concat_axis=0, tiled=True)  13 us
    all_gather x1, waiting for transfers between devices, body(): full_rows = lax.all_gather(tokens, 'tp', axis=1, tiled=True)  11.7 us
    all_to_all x1, starting transfers between devices, body(): lax.all_to_all(jnp.take(fresh_share, sources, axis=0), 'seq', split_axis=...  11.5 us
    sub x1, matrix products, body(): weights = jnp.exp(scores - top)  10.7 us
    all_to_all x1, waiting for transfers between devices, body(): lax.all_to_all(old_cache, 'seq', split_axis=0, concat_axis=0, tiled=True)  10.4 us
    reduce_scatter x1, waiting for transfers between devices, body(): lax.psum_scatter(partial_out.astype(jnp.bfloat16), 'tp', scatter_dimensio...  8.03 us
  transfers between devices with their start and end apart: 5, of which 5 were waited for; matrix products, arithmetic and copies ran while one was open for 7% of the time, Pallas kernels for 0%

commit v1 on v0

--- a/solution.py
+++ b/solution.py
@@ -1,3 +1,4 @@
+import functools
 import jax
 import jax.numpy as jnp
 from jax import lax
@@ -5,6 +6,28 @@
 
 EPSILON = 1e-05
 MASKED = -1e30
+
+
+def _enter_blocks(original, row_axis, d0):
+    full_n = lax.axis_size(row_axis)
+    parts_seen = tuple(((rr, (rr + 1) % full_n) for rr in range(full_n)))
+    in_order = tuple(((rr, (rr - 1) % full_n) for rr in range(full_n)))
+    met_up, y = ([original], [original])
+    for _ in range(full_n // 2):
+        met_up.append(lax.ppermute(met_up[-1], axis_name=row_axis, perm=parts_seen))
+    p = 0
+    while p < (full_n - 1) // 2:
+        y.append(lax.ppermute(y[-1], perm=in_order, axis_name=row_axis))
+        p = p + 1
+    carry_in = jnp.roll(
+        jnp.concatenate([*met_up[::-1], *y[1:]], axis=d0),
+        shift=(lax.axis_index(row_axis) - full_n // 2) * original.shape[d0],
+        axis=d0,
+    )
+    return carry_in
+
+
+direct_patches = functools.partial(_enter_blocks, row_axis="tp", d0=1)
 
 
 def normalize(rows, norm_gain):
@@ -40,7 +63,7 @@
     capacity = groups * block_rows
     arrived = lax.all_to_all(old_cache, "seq", split_axis=0, concat_axis=0, tiled=True)
     cache_share = jnp.take(arrived, holders, axis=0)
-    full_rows = lax.all_gather(tokens, "tp", axis=1, tiled=True)
+    full_rows = direct_patches(tokens)
     normed = normalize(full_rows, norm_gain)
     query = jnp.dot(normed, w_query, preferred_element_type=jnp.float32).astype(jnp.bfloat16)
     keyval = jnp.dot(normed, w_keyval, preferred_element_type=jnp.float32).astype(jnp.bfloat16)

time: 154 us -> 148 us (0.961)
  waiting for transfers between devices: 65.4 us -> 54 us
  local copies, waits for them, and re-layouts: 5.21 us -> 10.3 us
  starting transfers between devices: 24.8 us -> 28.3 us
  other arithmetic: 17 us -> 13.6 us
    all_gather x1 -> x0, waiting for transfers between devices: 11.7 us -> none  [body(): full_rows = lax.all_gather(tokens, 'tp', axis=1, tiled=True)]
    unnamed x17 -> x22, local copies, waits for them, and re-layouts: 1.35 us -> 6.43 us
    ppermute x0 -> x3, starting transfers between devices: none -> 3.9 us  [the longest x2 2.37 us: _enter_blocks(): met_up.append(lax.ppermute(met_up[-1], axis_name=row_axis, perm=parts_seen))]
    ppermute x0 -> x3, waiting for transfers between devices: none -> 2.43 us  [the longest x2 2.43 us: _enter_blocks(): met_up.append(lax.ppermute(met_up[-1], axis_name=row_axis, perm=parts_seen))]
    reduce_sum x1, other arithmetic: 2.09 us -> 0.36 us  [normalize(): average = jnp.mean(values, axis=1, keepdims=True)]
    reduce_sum x1, other arithmetic: 2.27 us -> 0.69 us  [normalize(): spread = jnp.mean(centred * centred, axis=1, keepdims=True)]
  transfers between devices with their start and end apart: 5 -> 7, of which waited for: 5 -> 5; matrix products, arithmetic and copies ran while one was open for 7% -> 10% of each run, Pallas kernels for 0% -> 0%
where the time goes in v1:
time: 148 us
  waiting for transfers between devices  54 us (36%)
  starting transfers between devices  28.3 us (19%)
  matrix products  25.7 us (17%)
  between operations  15.6 us (11%)
  other arithmetic  13.6 us (9%)
  local copies, waits for them, and re-layouts  10.3 us (7%)
    all_gather x1, waiting for transfers between devices, body(): lax.all_gather(cache_share, 'tp', axis=1, tiled=True)  20.8 us
    all_to_all x1, waiting for transfers between devices, body(): lax.all_to_all(jnp.take(fresh_share, sources, axis=0), 'seq', split_axis=...  13.2 us
    all_to_all x1, starting transfers between devices, body(): lax.all_to_all(old_cache, 'seq', split_axis=0, concat_axis=0, tiled=True)  12.6 us
    all_to_all x1, starting transfers between devices, body(): lax.all_to_all(jnp.take(fresh_share, sources, axis=0), 'seq', split_axis=...  11.5 us
    sub x1, matrix products, body(): weights = jnp.exp(scores - top)  10.7 us
    all_to_all x1, waiting for transfers between devices, body(): lax.all_to_all(old_cache, 'seq', split_axis=0, concat_axis=0, tiled=True)  9.44 us
    reduce_scatter x1, waiting for transfers between devices, body(): lax.psum_scatter(partial_out.astype(jnp.bfloat16), 'tp', scatter_dimensio...  8.13 us
    dot_general x1, matrix products, body(): jnp.einsum('htk,kd->thd', probs, values, preferred_element_type=jnp.float32)  7.05 us
  transfers between devices with their start and end apart: 7, of which 5 were waited for; matrix products, arithmetic and copies ran while one was open for 10% of the time, Pallas kernels for 0%

profile of v1, /device:TPU:1, one launch (start us, length us, event | category | flops | bytes accessed | tf_op | source)
XLA Modules:
  0.0 147.6 jit_solution(7710496070071526802)
XLA Ops:
  7.2 2.2 %collective-permute-start = (bf16[512,512]{1,0:T(8,128)(2,1)}, bf16[512,512]{1,0:T(8,128)(2,1)}, u32[]{:S(2)}, u32[]{:S(2)}) collective-permute-start(bf16[512,512]{1,0:T(8,128)(2,1)} %param.12), channel_id=1, source_target_pairs={{0,1},{1,2},{2,3},{3,0},{4,5},{5,6},{6,7},{7,4},{8,9},{9,10},{10,1... | collective-permute-start | bytes 1572872 | tf_op jit(solution)/shard_map/ppermute | solution.py:17
  9.4 1.5 %collective-permute-start.2 = (bf16[512,512]{1,0:T(8,128)(2,1)}, bf16[512,512]{1,0:T(8,128)(2,1)S(1)}, u32[]{:S(2)}, u32[]{:S(2)}) collective-permute-start(bf16[512,512]{1,0:T(8,128)(2,1)} %param.12), channel_id=1, source_target_pairs={{0,3},{1,0},{2,1},{3,2},{4,7},{5,4},{6,5},{7,6},{8,11},{9,8},{10,9... | collective-permute-start | bytes 1572872 | tf_op jit(solution)/shard_map/ppermute | solution.py:20
  10.9 12.6 %all-to-all-start = ((bf16[64,8,256]{2,1,0:T(8,128)(2,1)}), bf16[64,8,256]{2,1,0:T(8,128)(2,1)S(1)}, u32[]{:S(2)}, u32[]{:S(2)}) async-start(bf16[64,8,256]{2,1,0:T(8,128)(2,1)} %param.21), calls=%async_computation | async-start | bytes 524288 | tf_op jit(solution)/shard_map/all_to_all | solution.py:64
  24.9 0.8 select_reduce_fusion
  25.9 0.7 compare_select_fusion
  26.6 0.7 compare_and_fusion.1
  27.2 9.4 %all-to-all-done = bf16[64,8,256]{2,1,0:T(8,128)(2,1)S(1)} async-done(((bf16[64,8,256]{2,1,0:T(8,128)(2,1)}), bf16[64,8,256]{2,1,0:T(8,128)(2,1)S(1)}, u32[]{:S(2)}, u32[]{:S(2)}) %all-to-all-start) | async-done | bytes 262176 | tf_op jit(solution)/shard_map/all_to_all | solution.py:64
  36.7 1.3 gather_fusion
  38.0 2.4 %collective-permute-done.1 = bf16[512,512]{1,0:T(8,128)(2,1)} collective-permute-done((bf16[512,512]{1,0:T(8,128)(2,1)}, bf16[512,512]{1,0:T(8,128)(2,1)}, u32[]{:S(2)}, u32[]{:S(2)}) %collective-permute-start.1) | collective-permute-done | bytes 524320 | tf_op jit(solution)/shard_map/ppermute | solution.py:17
  40.4 1.1 constant_dynamic-update-slice_fusion.7
  41.5 1.1 constant_dynamic-update-slice_fusion.6
  42.6 1.1 constant_dynamic-update-slice_fusion.5
  43.8 1.2 constant_dynamic-update-slice_fusion.3
  45.0 1.1 constant_dynamic-update-slice_fusion.2
  46.6 0.7 fusion.8
  47.3 0.8 convolution_convert_fusion.2
  48.2 1.9 %dynamic_update_slice.3 = bf16[2048,256]{1,0:T(8,128)(2,1)S(1)} dynamic-update-slice(bf16[2048,256]{1,0:T(8,128)(2,1)S(1)} %broadcast.105, bf16[512,256]{1,0:T(8,128)(2,1)S(1)} %convolution_convert_fusion.2, s32[]{:T(128)S(6)} %select_n.54, s32[]{:T(128)} %constant.22.clone.1) | dynamic-update-slice | bytes 524292 | tf_op jit(solution)/shard_map/dynamic_update_slice | solution.py:70
  50.1 1.9 %select_select_fusion = (bf16[64,8,256]{2,1,0:T(8,128)(2,1)S(1)}, bf16[64,8,256]{2,1,0:T(8,128)(2,1)}) fusion(bf16[64,32,256]{2,1,0:T(8,128)(2,1)S(1)} %bitcast.55, s32[]{:T(128)S(6)} %select_n.59, pred[64,8]{1,0:T(8,128)(4,1)S(1)} %get-tuple-element.6, pred[64,8]{1,0:T(8,128)(4,1)S(1)} %get-tuple-element.5, bf16[64,8,256]{2,1,0:T(8,128)(2,1)} %gather_fusion, ...), kind=kLoop, calls=%fused_computation.29 | loop fusion | flops 393216 | bytes 1049668 | tf_op jit(solution)/shard_map/jit(_where)/select_n | solution.py:81
  52.3 1.8 %iota_compare_fusion = pred[512,2048]{0,1:T(8,128)(4,1)} fusion(s32[512]{0:T(512)S(1)} %iota_add_fusion.1), kind=kLoop, calls=%fused_computation.18 | loop fusion | flops 1048576 | bytes 1050624 | tf_op jit(solution)/shard_map/le | solution.py:111
  54.1 4.5 %convolution_convert_fusion.1 = bf16[512,512]{0,1:T(8,128)(2,1)} fusion(bf16[2048,512]{1,0:T(8,128)(2,1)} %param.14, f32[2048]{0:T(1024)S(1)} %copy-done.6, f32[512]{0:T(512)S(1)} %add_rsqrt_fusion, f32[512]{0:T(512)S(1)} %broadcast_multiply_fusion, bf16[512,4096]{1,0:T(8,128)(2,1)} %copy-done.1, s32[]{:T(128)S(6)} %select_n.53), kind=kOutput, calls=%fused_computation.21 | convolution fusion | flops 1079246848 | bytes 4730884 | tf_op jit(solution)/shard_map/dot_general | solution.py:68
  58.6 20.8 %all-gather.2.cloned.1.call-done = bf16[64,32,256]{2,1,0:T(8,128)(2,1)} async-done(((bf16[64,8,256]{2,1,0:T(8,128)(2,1)}), bf16[64,32,256]{2,1,0:T(8,128)(2,1)}) %all-gather.2.cloned.1.call-update) | async-done | bytes 1048592 | tf_op jit(solution)/shard_map/all_gather | solution.py:94
  79.4 3.8 %bitcast_select_fusion.4 = bf16[2048,256]{1,0:T(8,128)(2,1)} fusion(bf16[64,32,256]{2,1,0:T(8,128)(2,1)} %all-gather.2.cloned.1.call-done, bf16[2048,256]{1,0:T(8,128)(2,1)S(1)} %dynamic_update_slice.3, pred[2048]{0:T(1024)(128)(4,1)S(1)} %get-tuple-element.11, pred[2048]{0:T(1024)(128)(4,1)S(1)} %get-tuple-element.12), kind=kLoop, calls=%fused_computation.24 | loop fusion | flops 1048576 | bytes 3149824 | tf_op jit(solution)/shard_map/jit(_where)/select_n | solution.py:96
  83.2 10.7 %fusion.21 = (f32[4,512]{1,0:T(4,128)S(1)}, f32[4,512,2048]{1,2,0:T(8,128)}) fusion(pred[512,2048]{0,1:T(8,128)(4,1)} %iota_compare_fusion, bf16[512,4,128]{0,2,1:T(8,128)(2,1)} %bitcast.57, bf16[2048,256]{1,0:T(8,128)(2,1)} %bitcast_select_fusion.4), kind=kOutput, calls=%fused_computation.60 | convolution fusion | flops 1090521088 | bytes 18882560 | tf_op jit(solution)/shard_map/sub | solution.py:114
  93.9 7.0 %fusion.13 = bf16[128,4,512]{2,0,1:T(8,128)(2,1)S(1)} fusion(f32[4,512,2048]{1,2,0:T(8,128)} %get-tuple-element.8, f32[4,512]{1,0:T(4,128)S(1)} %get-tuple-element.7, bf16[2048,256]{1,0:T(8,128)(2,1)S(1)} %copy-done.4), kind=kOutput, calls=%fused_computation.22 | convolution fusion | flops 1082392576 | bytes 17833984 | tf_op jit(solution)/shard_map/htk,kd->thd/dot_general | solution.py:116
  101.0 2.6 %convolution_convert_fusion = bf16[512,2048]{1,0:T(8,128)(2,1)} fusion(bf16[512,512]{0,1:T(8,128)(2,1)S(1)} %bitcast.58, bf16[512,2048]{1,0:T(8,128)(2,1)S(1)} %copy-done), kind=kOutput, calls=%fused_computation.19 | convolution fusion | flops 1074790400 | bytes 4718592 | tf_op jit(solution)/shard_map/dot_general | solution.py:120
  103.7 0.6 gather_fusion.1
  104.3 0.8 broadcast_select_fusion
  105.2 11.5 %all-to-all-start.1 = ((bf16[64,8,256]{2,1,0:T(8,128)(2,1)}), bf16[64,8,256]{2,1,0:T(8,128)(2,1)S(1)}, u32[]{:S(2)}, u32[]{:S(2)}) async-start(bf16[64,8,256]{2,1,0:T(8,128)(2,1)} %broadcast_select_fusion), calls=%async_computation.2 | async-start | bytes 524288 | tf_op jit(solution)/shard_map/all_to_all | solution.py:91
  116.7 13.2 %all-to-all-done.1 = bf16[64,8,256]{2,1,0:T(8,128)(2,1)S(1)} async-done(((bf16[64,8,256]{2,1,0:T(8,128)(2,1)}), bf16[64,8,256]{2,1,0:T(8,128)(2,1)S(1)}, u32[]{:S(2)}, u32[]{:S(2)}) %all-to-all-start.1) | async-done | bytes 262176 | tf_op jit(solution)/shard_map/all_to_all | solution.py:91
  129.9 8.1 %reduce-scatter.2.cloned.1.call-done = bf16[512,512]{1,0:T(8,128)(2,1)} async-done(((bf16[512,2048]{1,0:T(8,128)(2,1)}), bf16[512,512]{1,0:T(8,128)(2,1)}) %reduce-scatter.2.cloned.1.call-update) | async-done | bytes 524304 | tf_op jit(solution)/shard_map/reduce_scatter | solution.py:121
  138.0 2.0 %select_convert_fusion = bf16[512,512]{1,0:T(8,128)(2,1)} fusion(bf16[512,512]{1,0:T(8,128)(2,1)} %reduce-scatter.2.cloned.1.call-done, bf16[512,512]{1,0:T(8,128)(2,1)S(1)} %copy-done.3, pred[512]{0:T(512)(128)(4,1)S(1)} %iota_compare_fusion.4), kind=kLoop, calls=%fused_computation.25 | loop fusion | flops 1310720 | bytes 1573376 | tf_op jit(solution)/shard_map/convert_element_type | solution.py:125
  140.0 0.7 copy.36
  (36 shorter events, 1.3 us)
Async XLA Ops:
  7.2 93.8 %copy-start = (bf16[512,2048]{1,0:T(8,128)(2,1)S(1)}, bf16[512,2048]{1,0:T(8,128)(2,1)}, u32[]{:S(2)}) copy-start(bf16[512,2048]{1,0:T(8,128)(2,1)} %param.16) | copy-start | bytes 6291460
  7.2 38.9 %copy-start.2 = (bf16[512,512]{1,0:T(8,128)(2,1)S(1)}, bf16[512,512]{1,0:T(8,128)(2,1)}, u32[]{:S(2)}) copy-start(bf16[512,512]{1,0:T(8,128)(2,1)} %param.12) | copy-start | bytes 1572868
  7.2 18.5 %collective-permute-start = (bf16[512,512]{1,0:T(8,128)(2,1)}, bf16[512,512]{1,0:T(8,128)(2,1)}, u32[]{:S(2)}, u32[]{:S(2)}) collective-permute-start(bf16[512,512]{1,0:T(8,128)(2,1)} %param.12), channel_id=1, source_target_pairs={{0,1},{1,2},{2,3},{3,0},{4,5},{5,6},{6,7},{7,4},{8,9},{9,10},{10,1... | collective-permute-start | bytes 1572872 | tf_op jit(solution)/shard_map/ppermute | solution.py:17
  9.4 34.3 %collective-permute-start.2 = (bf16[512,512]{1,0:T(8,128)(2,1)}, bf16[512,512]{1,0:T(8,128)(2,1)S(1)}, u32[]{:S(2)}, u32[]{:S(2)}) collective-permute-start(bf16[512,512]{1,0:T(8,128)(2,1)} %param.12), channel_id=1, source_target_pairs={{0,3},{1,0},{2,1},{3,2},{4,7},{5,4},{6,5},{7,6},{8,11},{9,8},{10,9... | collective-permute-start | bytes 1572872 | tf_op jit(solution)/shard_map/ppermute | solution.py:20
  10.9 25.7 %all-to-all-start = ((bf16[64,8,256]{2,1,0:T(8,128)(2,1)}), bf16[64,8,256]{2,1,0:T(8,128)(2,1)S(1)}, u32[]{:S(2)}, u32[]{:S(2)}) async-start(bf16[64,8,256]{2,1,0:T(8,128)(2,1)} %param.21), calls=%async_computation | async-start | bytes 524288 | tf_op jit(solution)/shard_map/all_to_all | solution.py:64
  23.5 55.9 %all-gather.2.cloned.1.call-start = ((), (), s32[]{:S(2)}) async-start(), calls=%async_computation.3 | async-start | bytes 1310720 | tf_op jit(solution)/shard_map/all_gather | solution.py:94
  25.7 14.6 %collective-permute-start.1 = (bf16[512,512]{1,0:T(8,128)(2,1)}, bf16[512,512]{1,0:T(8,128)(2,1)}, u32[]{:S(2)}, u32[]{:S(2)}) collective-permute-start(bf16[512,512]{1,0:T(8,128)(2,1)} %collective-permute-done), channel_id=1, source_target_pairs={{0,1},{1,2},{2,3},{3,0},{4,5},{5,6},{6,7},{7,4},{8,9},{9,10},{10,1... | collective-permute-start | bytes 1572872 | tf_op jit(solution)/shard_map/ppermute | solution.py:17
  43.8 3.5 %copy-start.5 = (bf16[2048,256]{1,0:T(8,128)(2,1)S(1)}, bf16[2048,256]{1,0:T(8,128)(2,1)}, u32[]{:S(2)}) copy-start(bf16[2048,256]{1,0:T(8,128)(2,1)} %param.15) | copy-start | bytes 3145732
  43.8 3.5 %copy-start.6 = (f32[2048]{0:T(1024)S(1)}, f32[2048]{0:T(1024)}, u32[]{:S(2)}) copy-start(f32[2048]{0:T(1024)} %param.13) | copy-start | bytes 24580
  46.2 1.9 %copy-start.1 = (bf16[512,4096]{1,0:T(8,128)(2,1)}, bf16[512,4096]{1,0:T(8,128)(2,1)S(1)}, u32[]{:S(2)}) copy-start(bf16[512,4096]{1,0:T(8,128)(2,1)S(1)} %constant_dynamic-update-slice_fusion) | copy-start | bytes 12582916
  52.1 85.9 %reduce-scatter.2.cloned.1.call-start = ((), (), s32[]{:S(2)}) async-start(), calls=%async_computation.4 | async-start | bytes 2621440 | tf_op jit(solution)/shard_map/reduce_scatter | solution.py:121
  83.2 10.7 %copy-start.4 = (bf16[2048,256]{1,0:T(8,128)(2,1)S(1)}, bf16[2048,256]{1,0:T(8,128)(2,1)}, u32[]{:S(2)}) copy-start(bf16[2048,256]{1,0:T(8,128)(2,1)} %bitcast_select_fusion.4) | copy-start | bytes 3145732
  101.0 37.0 %copy-start.3 = (bf16[512,512]{1,0:T(8,128)(2,1)S(1)}, bf16[512,512]{1,0:T(8,128)(2,1)}, u32[]{:S(2)}) copy-start(bf16[512,512]{1,0:T(8,128)(2,1)} %param.12) | copy-start | bytes 1572868
  105.2 24.7 %all-to-all-start.1 = ((bf16[64,8,256]{2,1,0:T(8,128)(2,1)}), bf16[64,8,256]{2,1,0:T(8,128)(2,1)S(1)}, u32[]{:S(2)}, u32[]{:S(2)}) async-start(bf16[64,8,256]{2,1,0:T(8,128)(2,1)} %broadcast_select_fusion), calls=%async_computation.2 | async-start | bytes 524288 | tf_op jit(solution)/shard_map/all_to_all | solution.py:91
Sparse Core Ops, SparseCore 0:
  52.2 27.1 all-gather.1
  103.8 34.1 reduce-scatter.1
